TPU v7x, 32 devices: a whole 2x2x4 slice. The times are simulated.
32 devices in a mesh: row: 8 (over y, x, core), col: 4 (over z).
Axes of the slice: x: 2, y: 2, z: 4, core: 2. Of those that a mesh axis runs over, the one named last changes fastest.
Arguments:
- skew_matrix: float32 [16384, 16384], P('row', 'col'), may hold values from -80 to 80, as said below
- first_reflector: float32 [16384, 128], P('row'), may hold values from -0.05625 to 0.05625
- first_factor: float32 [128, 128], replicated, may hold values from -0.6 to 1.5, as said below
- second_reflector: float32 [16384, 128], P('row'), may hold values from -0.05625 to 0.05625
- second_factor: float32 [128, 128], replicated, may hold values from -0.6 to 1.5, as said below
- vectors: float32 [16384, 4096], P('row', 'col'), may hold values from -6 to 6
Outputs:
- updated_matrix: float32 [16384, 16384], P('row', 'col')
- back_vectors: float32 [16384, 4096], P('row', 'col')
Inputs may be any that keep to these rules, and one draw needn't show every extreme that they name: skew_matrix is skew-symmetric: entry (i, j) equals minus entry (j, i) exactly. first_factor is upper triangular with a positive diagonal. second_factor is upper triangular with a positive diagonal.
All inputs are finite; a program needn't handle non-finite values.
Results may differ from a plain program's by a relative error of at most 0.000059.
Values sent between devices are 32-bit elements; how exact they have to be, the bound alone decides.
A program may use at most 192 MiB of HBM per device.

v0:
```python
import jax
import jax.numpy as jnp
from jax import lax
from jax.sharding import PartitionSpec as P


def multiply(left, right):
    return jnp.dot(left, right, precision=lax.Precision.HIGHEST, preferred_element_type=jnp.float32)


def inner_rows(left, right):
    return lax.dot_general(
        left,
        right,
        (((0,), (0,)), ((), ())),
        precision=lax.Precision.HIGHEST,
        preferred_element_type=jnp.float32,
    )


def transform(matrix, own_rows, col_rows, factor):
    partial_rows = multiply(matrix, col_rows)
    summed_rows = lax.psum(partial_rows, "col")
    partial_cols = inner_rows(matrix, own_rows)
    summed_cols = lax.psum(partial_cols, "row")
    plain_cols = -summed_cols
    gram = lax.psum(inner_rows(own_rows, summed_rows), "row")
    correction = multiply(multiply(factor.T, gram), factor)
    fixed_rows = multiply(summed_rows, factor) - 0.5 * multiply(own_rows, correction)
    fixed_cols = multiply(plain_cols, factor) - 0.5 * multiply(col_rows, correction)
    left = jnp.concatenate([own_rows, -fixed_rows], axis=1)
    right = jnp.concatenate([fixed_cols, col_rows], axis=1)
    update = lax.dot_general(
        left,
        right,
        (((1,), (1,)), ((), ())),
        precision=lax.Precision.HIGHEST,
        preferred_element_type=jnp.float32,
    )
    return matrix + update


def shards(skew_matrix, first_reflector, first_factor, second_reflector, second_factor, vectors):
    joined = jnp.concatenate([first_reflector, second_reflector], axis=1)
    correlation, projected = lax.psum(
        (inner_rows(first_reflector, second_reflector), inner_rows(joined, vectors)), "row"
    )
    top_right = -multiply(multiply(first_factor, correlation), second_factor)
    zeros_block = jnp.zeros_like(second_factor)
    compact = jnp.concatenate(
        [
            jnp.concatenate([first_factor, top_right], axis=1),
            jnp.concatenate([zeros_block, second_factor], axis=1),
        ],
        axis=0,
    )
    back_vectors = vectors - multiply(joined, multiply(compact, projected))
    cols_here = skew_matrix.shape[1]
    col_index = lax.axis_index("col")
    whole_first, whole_second = (
        lax.all_gather(first_reflector, "row", axis=0, tiled=True),
        lax.all_gather(second_reflector, "row", axis=0, tiled=True),
    )
    col_start = col_index * cols_here
    panel_first = lax.dynamic_slice_in_dim(whole_first, col_start, cols_here, 0)
    panel_second = lax.dynamic_slice_in_dim(whole_second, col_start, cols_here, 0)
    inner = transform(skew_matrix, first_reflector, panel_first, first_factor)
    updated_matrix = transform(inner, second_reflector, panel_second, second_factor)
    return (updated_matrix, back_vectors)


def solution(mesh):
    in_specs = (P("row", "col"), P("row", None), P(), P("row", None), P(), P("row", "col"))
    out_specs = (P("row", "col"), P("row", "col"))
    return jax.shard_map(shards, mesh=mesh, in_specs=in_specs, out_specs=out_specs, check_vma=False)
```

profile of v0, /device:TPU:0, one launch (start us, length us, event | category | flops | bytes accessed | tf_op | source)
XLA Modules:
  0.0 549.0 jit_solution(17140156105039725318)
XLA Ops:
  7.2 0.0 all-gather.3.cloned.1.call-start
  7.2 0.7 all-gather.3.cloned.1.call-update
  7.9 0.0 all-reduce.8.cloned.1.call-start
  7.9 58.9 %all-gather.3.cloned.1.call-done = f32[16384,128]{1,0:T(8,128)} async-done(((f32[2048,128]{1,0:T(8,128)}), f32[16384,128]{1,0:T(8,128)}) %all-gather.3.cloned.1.call-update) | async-done | bytes 8388624 | tf_op jit(solution)/shard_map/all_gather | solution.py:61
  66.9 1.7 constant_dynamic-slice_fusion.1
  68.6 0.0 copy-start.4
  68.6 1.3 copy-done.4
  69.9 41.9 %convolution_bitcast_fusion = f32[2048,128]{0,1:T(8,128)} fusion(f32[4096,128]{1,0:T(8,128)S(1)} %constant_dynamic-slice_fusion.1, f32[2048,4096]{1,0:T(8,128)} %param.6), kind=kOutput, calls=%fused_computation.13 | convolution fusion | flops 12884901888 | bytes 36700160 | tf_op jit(solution)/shard_map/dot_general | solution.py:8
  111.8 0.0 copy-start
  111.8 0.0 copy-start.1
  111.8 0.0 all-reduce.8.cloned.1.call-update
  111.8 0.0 all-gather.5.cloned.1.call-start
  111.9 0.7 all-gather.5.cloned.1.call-update
  112.6 0.0 all-reduce.14.cloned.1.call-start
  112.6 0.4 copy-done
  113.0 1.1 constant_dynamic-update-slice_fusion.1
  114.1 0.0 copy-done.1
  114.1 1.1 constant_dynamic-update-slice_fusion
  115.2 57.1 %fusion.39 = f32[4096,128]{1,0:T(8,128)} fusion(f32[2048,4096]{1,0:T(8,128)} %param.6, f32[2048,128]{1,0:T(8,128)S(1)} %copy-done), kind=kOutput, calls=%fused_computation.56 | convolution fusion | flops 12884901888 | bytes 36700160 | tf_op jit(solution)/shard_map/dot_general | solution.py:12
  172.3 0.0 all-reduce.8.cloned.1.call-done
  172.3 3.1 convolution_bitcast_fusion.2
  175.4 0.0 all-reduce.14.cloned.1.call-update
  175.4 0.0 all-reduce.10.cloned.1.call-start
  175.5 11.1 %fusion.47 = f32[256,1024]{1,0:T(8,128)} fusion(f32[2048,256]{1,0:T(8,128)} %constant_dynamic-update-slice_fusion, f32[2048,1024]{1,0:T(8,128)} %param.11), kind=kOutput, calls=%fused_computation.64 | convolution fusion | flops 6442450944 | bytes 11534336 | tf_op jit(solution)/shard_map/dot_general | solution.py:12
  186.5 2.4 fusion.45
  189.0 30.4 %all-gather.5.cloned.1.call-done = f32[16384,128]{1,0:T(8,128)} async-done(((f32[2048,128]{1,0:T(8,128)}), f32[16384,128]{1,0:T(8,128)}) %all-gather.5.cloned.1.call-update) | async-done | bytes 8388624 | tf_op jit(solution)/shard_map/all_gather | solution.py:62
  219.3 3.2 constant_dynamic-slice_fusion
  222.6 0.0 copy-done.8
  222.6 0.0 copy-done.6
  222.6 1.8 fusion.36
  224.4 60.9 %all-reduce.14.cloned.1.call-done = (f32[4096,128]{1,0:T(8,128)}, f32[128,128]{0,1:T(8,128)}) async-done(((f32[4096,128]{1,0:T(8,128)}, f32[128,128]{0,1:T(8,128)}), (f32[4096,128]{1,0:T(8,128)}, f32[128,128]{0,1:T(8,128)})) %all-reduce.14.cloned.1.call-update) | async-done | bytes 2162704 | tf_op jit(solution)/shard_map/psum | solution.py:25
  285.3 3.6 fusion.22
  288.9 0.0 copy-done.12
  288.9 0.2 fusion.37
  289.1 0.3 fusion.38
  289.4 0.0 copy-done.5
  289.4 1.9 fusion.1
  291.3 1.0 fusion.13
  292.3 0.0 copy-start.2
  292.3 33.7 %convolution_add_fusion.1 = f32[2048,4096]{1,0:T(8,128)} fusion(f32[2048,4096]{1,0:T(8,128)} %param.6, f32[4096,128]{1,0:T(8,128)S(1)} %copy-done.5, f32[4096,128]{1,0:T(8,128)S(1)} %fusion.1, f32[2048,128]{1,0:T(8,128)S(1)} %fusion.13, f32[2048,128]{1,0:T(8,128)S(1)} %copy-done), kind=kOutput, calls=%fused_computation.1 | convolution fusion | flops 25779765248 | bytes 73400320 | tf_op jit(solution)/shard_map/dot_general | solution.py:33
  325.9 0.0 copy-done.2
  325.9 30.9 %fusion.40 = f32[2048,128]{1,0:T(8,128)} fusion(f32[2048,4096]{1,0:T(8,128)} %convolution_add_fusion.1, f32[4096,128]{1,0:T(8,128)S(1)} %copy-done.2), kind=kOutput, calls=%fused_computation.57 | convolution fusion | flops 12884901888 | bytes 36700160 | tf_op jit(solution)/shard_map/dot_general | solution.py:8
  356.8 0.0 all-reduce.10.cloned.1.call-update
  356.8 0.0 all-reduce.12.cloned.1.call-start
  356.9 57.1 %fusion.44 = f32[4096,128]{1,0:T(8,128)} fusion(f32[2048,4096]{1,0:T(8,128)} %convolution_add_fusion.1, f32[2048,128]{1,0:T(8,128)S(1)} %copy-done.1), kind=kOutput, calls=%fused_computation.61 | convolution fusion | flops 12884901888 | bytes 36700160 | tf_op jit(solution)/shard_map/dot_general | solution.py:12
  414.0 0.0 all-reduce.10.cloned.1.call-done
  414.0 3.7 convolution_bitcast_fusion.1
  417.7 0.0 all-reduce.12.cloned.1.call-update
  417.7 1.2 copy-done.7
  418.9 0.0 copy-done.9
  418.9 1.0 fusion.41
  419.9 68.0 %all-reduce.12.cloned.1.call-done = (f32[4096,128]{1,0:T(8,128)}, f32[128,128]{0,1:T(8,128)}, f32[256,1024]{1,0:T(8,128)}, f32[128,128]{1,0:T(8,128)}) async-done(((f32[4096,128]{1,0:T(8,128)}, f32[128,128]{0,1:T(8,128)}, f32[256,1024]{1,0:T(8,128)}, f32[128,128]{1,0:T(8,128)}), (f32[4096,128]{1,0:T(8,128)}, f32[128,128]{0,1:T(8,128)}, f32[256,1024]{1,0:T(8,128)}, ...) | async-done | bytes 3276816 | tf_op jit(solution)/shard_map/psum | solution.py:25
  487.9 3.6 fusion.20
  491.4 0.0 copy-done.13
  491.5 0.2 fusion.42
  491.7 0.3 fusion.43
  492.0 0.0 copy-done.3
  492.0 1.9 fusion
  493.9 1.0 fusion.10
  494.9 0.3 fusion.46
  495.2 0.3 convolution_negate_fusion
  495.5 1.0 fusion.24
  496.5 12.2 %convolution_subtract_fusion = f32[2048,1024]{1,0:T(8,128)} fusion(f32[2048,1024]{1,0:T(8,128)} %param.11, f32[2048,256]{1,0:T(8,128)} %constant_dynamic-update-slice_fusion, f32[256,1024]{1,0:T(8,128)S(1)} %fusion.24), kind=kOutput, calls=%fused_computation.6 | convolution fusion | flops 6444548096 | bytes 19922944 | tf_op jit(solution)/shard_map/dot_general | solution.py:8
  508.7 33.0 %convolution_add_fusion = f32[2048,4096]{1,0:T(8,128)} fusion(f32[2048,4096]{1,0:T(8,128)} %convolution_add_fusion.1, f32[4096,128]{1,0:T(8,128)S(1)} %copy-done.3, f32[4096,128]{1,0:T(8,128)S(1)} %fusion, f32[2048,128]{1,0:T(8,128)S(1)} %fusion.10, f32[2048,128]{1,0:T(8,128)S(1)} %copy-done.1), kind=kOutput, calls=%fused_computation | convolution fusion | flops 25779765248 | bytes 73400320 | tf_op jit(solution)/shard_map/dot_general | solution.py:33
  (12 shorter events, 0.0 us)
Async XLA Ops:
  7.2 59.7 %all-gather.3.cloned.1.call-start = ((), (), s32[]{:S(2)}) async-start(), calls=%async_computation | async-start | bytes 9437184 | tf_op jit(solution)/shard_map/all_gather | solution.py:61
  7.9 164.4 %all-reduce.8.cloned.1.call-start = ((), (), s32[]{:S(2)}) async-start(), calls=%async_computation.1 | async-start | bytes 2097152 | tf_op jit(solution)/shard_map/psum | solution.py:23
  68.6 1.3 copy-start.4
  111.8 1.2 copy-start
  111.8 2.3 copy-start.1
  111.8 107.5 %all-gather.5.cloned.1.call-start = ((), (), s32[]{:S(2)}) async-start(), calls=%async_computation.2 | async-start | bytes 9437184 | tf_op jit(solution)/shard_map/all_gather | solution.py:62
  112.6 172.7 %all-reduce.14.cloned.1.call-start = ((), (), s32[]{:S(2)}) async-start(), calls=%async_computation.5 | async-start | bytes 4325376 | tf_op jit(solution)/shard_map/psum | solution.py:25
  175.4 238.6 %all-reduce.10.cloned.1.call-start = ((), (), s32[]{:S(2)}) async-start(), calls=%async_computation.3 | async-start | bytes 2097152 | tf_op jit(solution)/shard_map/psum | solution.py:23
  189.0 33.6 %copy-start.8 = (f32[128,128]{1,0:T(8,128)S(1)}, f32[128,128]{1,0:T(8,128)}, u32[]{:S(2)}) copy-start(f32[128,128]{1,0:T(8,128)} %param.8) | copy-start | bytes 196612
  219.3 3.2 copy-start.6
  285.3 3.6 copy-start.12
  285.3 4.1 copy-start.5
  292.3 33.7 %copy-start.2 = (f32[4096,128]{1,0:T(8,128)S(1)}, f32[4096,128]{1,0:T(8,128)}, u32[]{:S(2)}) copy-start(f32[4096,128]{1,0:T(8,128)} %constant_dynamic-slice_fusion) | copy-start | bytes 6291460
  356.8 131.0 %all-reduce.12.cloned.1.call-start = ((), (), s32[]{:S(2)}) async-start(), calls=%async_computation.4 | async-start | bytes 6553600 | tf_op jit(solution)/shard_map/psum | solution.py:25
  417.7 1.2 copy-start.7
  417.7 1.2 copy-start.9
  487.9 3.6 copy-start.13
  487.9 4.1 copy-start.3
  493.8 1.0 copy-start.11
  493.9 1.6 copy-start.10
Sparse Core Ops, SparseCore 0:
  9.9 56.9 all-gather.2
  112.0 51.8 all-reduce.7
  165.8 53.5 all-gather.4
  223.1 62.1 all-reduce.13
  357.0 51.0 all-reduce.9
  417.8 70.0 all-reduce.11
where the time goes:
time: 559 us; the launch traced here: 549 us
  matrix products  304 us (54%)
  waiting for transfers between devices  220 us (39%)
  between operations  14.8 us (3%)
  local copies, waits for them, and re-layouts  10 us (2%)
    dot_general x6, matrix products, inner_rows(): lax.dot_general(left, right, (((0,), (0,)), ((), ())), precision=lax.Prec...  134 us
    psum x2, waiting for transfers between devices, transform(): summed_cols = lax.psum(partial_cols, 'row')  129 us
    dot_general x18, matrix products, multiply(): jnp.dot(left, right, precision=lax.Precision.HIGHEST, preferred_element_t...  103 us
    dot_general x2, matrix products, transform(): lax.dot_general(left, right, (((1,), (1,)), ((), ())), precision=lax.Prec...  66.7 us
    all_gather x1, waiting for transfers between devices, shards(): lax.all_gather(first_reflector, 'row', axis=0, tiled=True)  58.9 us
    all_gather x1, waiting for transfers between devices, shards(): lax.all_gather(second_reflector, 'row', axis=0, tiled=True)  30.4 us
  transfers between devices with their start and end apart: 6, of which 4 were waited for; matrix products, arithmetic and copies ran while one was open for 25% of the time, Pallas kernels for 0%

commit v1 on v0

--- a/solution.py
+++ b/solution.py
@@ -2,6 +2,18 @@
 import jax.numpy as jnp
 from jax import lax
 from jax.sharding import PartitionSpec as P
+
+
+def gather_by_bits(x, axis, dim):
+    ways, here, step = (lax.axis_size(axis), lax.axis_index(axis), x.shape[dim])
+    line, have = (x, 1)
+    while have < ways:
+        line = jnp.concatenate(
+            [line, lax.ppermute(line, axis, [(d, (d - have) % ways) for d in range(ways)])],
+            axis=dim,
+        )
+        have = 2 * have
+    return jnp.roll(line, here * step, axis=dim)
 
 
 def multiply(left, right):
@@ -59,7 +71,7 @@
     col_index = lax.axis_index("col")
     whole_first, whole_second = (
         lax.all_gather(first_reflector, "row", axis=0, tiled=True),
-        lax.all_gather(second_reflector, "row", axis=0, tiled=True),
+        gather_by_bits(second_reflector, "row", 0),
     )
     col_start = col_index * cols_here
     panel_first = lax.dynamic_slice_in_dim(whole_first, col_start, cols_here, 0)

time: 559 us -> 579 us (1.036)
  local copies, waits for them, and re-layouts: 10 us -> 28.1 us
  other arithmetic: 0 us -> 6.55 us
    ppermute x0 -> x3, waiting for transfers between devices: none -> 59.2 us  [gather_by_bits(): lax.ppermute(line, axis, [(d, (d - have) % ways) for d in range(ways)])]
    all_gather x1, waiting for transfers between devices: 58.9 us -> 0.01 us  [shards(): lax.all_gather(first_reflector, 'row', axis=0, tiled=True)]
    psum x2, waiting for transfers between devices: 0.04 us -> 36.9 us  [transform(): summed_rows = lax.psum(partial_rows, 'col')]
    all_gather x1 -> x0, waiting for transfers between devices: 30.4 us -> none  [shards(): lax.all_gather(second_reflector, 'row', axis=0, tiled=True)]
    unnamed x29 -> x37, local copies, waits for them, and re-layouts: 4.03 us -> 16.2 us
    psum x2, waiting for transfers between devices: 129 us -> 120 us  [transform(): summed_cols = lax.psum(partial_cols, 'row')]
    concatenate x0 -> x2, other arithmetic: none -> 6.55 us  [gather_by_bits(): jnp.concatenate([line, lax.ppermute(line, axis, [(d, (d - have) % ways) f...]
  transfers between devices with their start and end apart: 6 -> 8, of which waited for: 4 -> 6; matrix products, arithmetic and copies ran while one was open for 25% -> 36% of each run, Pallas kernels for 0% -> 0%
where the time goes in v1:
time: 579 us; the launch traced here: 573 us
  matrix products  303 us (52%)
  waiting for transfers between devices  217 us (37%)
  local copies, waits for them, and re-layouts  28.1 us (5%)
  between operations  14.3 us (2%)
  other arithmetic  6.55 us (1%)
    dot_general x6, matrix products, inner_rows(): lax.dot_general(left, right, (((0,), (0,)), ((), ())), precision=lax.Prec...  134 us
    psum x2, waiting for transfers between devices, transform(): summed_cols = lax.psum(partial_cols, 'row')  120 us
    dot_general x18, matrix products, multiply(): jnp.dot(left, right, precision=lax.Precision.HIGHEST, preferred_element_t...  103 us
    dot_general x2, matrix products, transform(): lax.dot_general(left, right, (((1,), (1,)), ((), ())), precision=lax.Prec...  66.6 us
    ppermute x3, waiting for transfers between devices, gather_by_bits(): lax.ppermute(line, axis, [(d, (d - have) % ways) for d in range(ways)])  59.2 us
    psum x2, waiting for transfers between devices, transform(): summed_rows = lax.psum(partial_rows, 'col')  36.9 us
    unnamed x37, local copies, waits for them, and re-layouts  16.2 us
  transfers between devices with their start and end apart: 8, of which 6 were waited for; matrix products, arithmetic and copies ran while one was open for 36% of the time, Pallas kernels for 0%

profile of v1, /device:TPU:0, one launch (start us, length us, event | category | flops | bytes accessed | tf_op | source)
XLA Modules:
  0.0 573.0 jit_solution(2641443353003448031)
XLA Ops:
  7.2 0.0 all-gather.2.cloned.1.call-start
  7.2 0.7 all-gather.2.cloned.1.call-update
  7.9 0.0 copy-start.1
  7.9 0.0 all-reduce.8.cloned.1.call-start
  8.0 3.4 collective-permute-start
  11.4 18.5 %collective-permute-done = f32[2048,128]{1,0:T(8,128)S(1)} collective-permute-done((f32[2048,128]{1,0:T(8,128)}, f32[2048,128]{1,0:T(8,128)S(1)}, u32[]{:S(2)}, u32[]{:S(2)}) %collective-permute-start) | collective-permute-done | bytes 1048608 | tf_op jit(solution)/shard_map/ppermute | solution.py:12
  29.9 2.7 pad_maximum_fusion.1
  32.6 0.0 collective-permute-start.1
  32.6 0.1 constant_dynamic-update-slice_fusion.9
  32.7 1.1 copy-done
  33.8 1.1 constant_dynamic-update-slice_fusion.8
  34.9 2.4 fusion.45
  37.3 10.3 %fusion.47 = f32[256,1024]{1,0:T(8,128)} fusion(f32[2048,256]{1,0:T(8,128)S(1)} %get-tuple-element.8, f32[2048,1024]{1,0:T(8,128)} %param.11), kind=kOutput, calls=%fused_computation.74 | convolution fusion | flops 6442450944 | bytes 11534336 | tf_op jit(solution)/shard_map/dot_general | solution.py:24
  47.7 32.6 %collective-permute-done.1 = f32[4096,128]{1,0:T(8,128)} collective-permute-done((f32[4096,128]{1,0:T(8,128)}, f32[4096,128]{1,0:T(8,128)}, u32[]{:S(2)}, u32[]{:S(2)}) %collective-permute-start.1) | collective-permute-done | bytes 2097184 | tf_op jit(solution)/shard_map/ppermute | solution.py:12
  80.2 3.9 pad_maximum_fusion
  84.1 0.6 collective-permute-start.2
  84.7 56.9 %fusion.39 = f32[4096,128]{1,0:T(8,128)} fusion(f32[2048,4096]{1,0:T(8,128)} %param.6, f32[2048,128]{1,0:T(8,128)S(1)} %copy-done.1), kind=kOutput, calls=%fused_computation.66 | convolution fusion | flops 12884901888 | bytes 36700160 | tf_op jit(solution)/shard_map/dot_general | solution.py:24
  141.6 1.0 constant_dynamic-update-slice_fusion.6
  142.6 3.0 constant_dynamic-update-slice_fusion.5
  145.7 3.0 constant_dynamic-slice_fusion.1
  148.7 42.6 %convolution_bitcast_fusion = f32[2048,128]{0,1:T(8,128)} fusion(f32[4096,128]{1,0:T(8,128)} %constant_dynamic-slice_fusion.1, f32[2048,4096]{1,0:T(8,128)} %param.6), kind=kOutput, calls=%fused_computation.14 | convolution fusion | flops 12884901888 | bytes 36700160 | tf_op jit(solution)/shard_map/dot_general | solution.py:20
  191.3 0.0 all-reduce.8.cloned.1.call-update
  191.4 0.0 all-reduce.14.cloned.1.call-start
  191.4 8.1 %collective-permute-done.2 = f32[8192,128]{1,0:T(8,128)} collective-permute-done((f32[8192,128]{1,0:T(8,128)}, f32[8192,128]{1,0:T(8,128)}, u32[]{:S(2)}, u32[]{:S(2)}) %collective-permute-start.2) | collective-permute-done | bytes 4194336 | tf_op jit(solution)/shard_map/ppermute | solution.py:12
  199.5 4.5 constant_dynamic-update-slice_fusion.4
  204.0 1.0 constant_dynamic-update-slice_fusion.3
  205.0 1.0 constant_dynamic-update-slice_fusion.2
  206.0 3.1 constant_dynamic-update-slice_fusion.1
  209.1 36.9 %all-reduce.8.cloned.1.call-done = f32[2048,128]{0,1:T(8,128)} async-done(((f32[2048,128]{0,1:T(8,128)}), f32[2048,128]{0,1:T(8,128)}) %all-reduce.8.cloned.1.call-update) | async-done | bytes 1048592 | tf_op jit(solution)/shard_map/psum | solution.py:35
  246.0 3.0 convolution_bitcast_fusion.2
  248.9 0.0 all-reduce.14.cloned.1.call-update
  249.0 0.0 all-reduce.10.cloned.1.call-start
  249.0 4.5 constant_dynamic-update-slice_fusion
  253.5 3.3 constant_dynamic-slice_fusion
  256.8 1.8 fusion.36
  258.6 52.2 %all-reduce.14.cloned.1.call-done = (f32[4096,128]{1,0:T(8,128)}, f32[128,128]{0,1:T(8,128)}) async-done(((f32[4096,128]{1,0:T(8,128)}, f32[128,128]{0,1:T(8,128)}), (f32[4096,128]{1,0:T(8,128)}, f32[128,128]{0,1:T(8,128)})) %all-reduce.14.cloned.1.call-update) | async-done | bytes 2162704 | tf_op jit(solution)/shard_map/psum | solution.py:37
  310.8 3.6 fusion.22
  314.3 0.2 fusion.37
  314.6 0.3 fusion.38
  314.9 1.9 fusion.1
  316.7 1.0 fusion.13
  317.7 0.0 copy-start.2
  317.7 33.4 %convolution_add_fusion.1 = f32[2048,4096]{1,0:T(8,128)} fusion(f32[2048,4096]{1,0:T(8,128)} %param.6, f32[4096,128]{1,0:T(8,128)S(1)} %copy-done.4, f32[4096,128]{1,0:T(8,128)S(1)} %fusion.1, f32[2048,128]{1,0:T(8,128)S(1)} %fusion.13, f32[2048,128]{1,0:T(8,128)S(1)} %copy-done.1), kind=kOutput, calls=%fused_computation.1 | convolution fusion | flops 25779765248 | bytes 73400320 | tf_op jit(solution)/shard_map/dot_general | solution.py:45
  351.1 30.9 %fusion.40 = f32[2048,128]{1,0:T(8,128)} fusion(f32[2048,4096]{1,0:T(8,128)} %convolution_add_fusion.1, f32[4096,128]{1,0:T(8,128)S(1)} %copy-done.2), kind=kOutput, calls=%fused_computation.67 | convolution fusion | flops 12884901888 | bytes 36700160 | tf_op jit(solution)/shard_map/dot_general | solution.py:20
  382.0 0.0 all-reduce.10.cloned.1.call-update
  382.0 0.0 all-reduce.12.cloned.1.call-start
  382.1 57.3 %fusion.44 = f32[4096,128]{1,0:T(8,128)} fusion(f32[2048,4096]{1,0:T(8,128)} %convolution_add_fusion.1, f32[2048,128]{1,0:T(8,128)S(1)} %copy-done), kind=kOutput, calls=%fused_computation.71 | convolution fusion | flops 12884901888 | bytes 36700160 | tf_op jit(solution)/shard_map/dot_general | solution.py:24
  439.4 0.0 all-reduce.10.cloned.1.call-done
  439.5 3.7 convolution_bitcast_fusion.1
  443.1 0.0 all-reduce.12.cloned.1.call-update
  443.2 1.2 copy-done.8
  444.4 1.0 fusion.41
  445.3 68.0 %all-reduce.12.cloned.1.call-done = (f32[4096,128]{1,0:T(8,128)}, f32[128,128]{0,1:T(8,128)}, f32[256,1024]{1,0:T(8,128)}, f32[128,128]{1,0:T(8,128)}) async-done(((f32[4096,128]{1,0:T(8,128)}, f32[128,128]{0,1:T(8,128)}, f32[256,1024]{1,0:T(8,128)}, f32[128,128]{1,0:T(8,128)}), (f32[4096,128]{1,0:T(8,128)}, f32[128,128]{0,1:T(8,128)}, f32[256,1024]{1,0:T(8,128)}, ...) | async-done | bytes 3276816 | tf_op jit(solution)/shard_map/psum | solution.py:37
  513.3 3.6 fusion.20
  517.0 0.2 fusion.42
  517.2 0.3 fusion.43
  517.5 1.9 fusion
  519.4 1.0 fusion.10
  520.4 0.3 fusion.46
  520.6 0.3 convolution_negate_fusion
  521.0 1.0 fusion.24
  522.0 0.0 copy-done.6
  522.0 11.0 %convolution_subtract_fusion = f32[2048,1024]{1,0:T(8,128)} fusion(f32[2048,1024]{1,0:T(8,128)} %param.11, f32[2048,256]{1,0:T(8,128)S(1)} %copy-done.6, f32[256,1024]{1,0:T(8,128)S(1)} %fusion.24), kind=kOutput, calls=%fused_computation.6 | convolution fusion | flops 6444548096 | bytes 19922944 | tf_op jit(solution)/shard_map/dot_general | solution.py:20
  533.0 33.2 %convolution_add_fusion = f32[2048,4096]{1,0:T(8,128)} fusion(f32[2048,4096]{1,0:T(8,128)} %convolution_add_fusion.1, f32[4096,128]{1,0:T(8,128)S(1)} %copy-done.3, f32[4096,128]{1,0:T(8,128)S(1)} %fusion, f32[2048,128]{1,0:T(8,128)S(1)} %fusion.10, f32[2048,128]{1,0:T(8,128)S(1)} %copy-done), kind=kOutput, calls=%fused_computation | convolution fusion | flops 25779765248 | bytes 73400320 | tf_op jit(solution)/shard_map/dot_general | solution.py:45
  (26 shorter events, 0.0 us)
Async XLA Ops:
  7.2 138.5 %all-gather.2.cloned.1.call-start = ((), (), s32[]{:S(2)}) async-start(), calls=%async_computation | async-start | bytes 9437184 | tf_op jit(solution)/shard_map/all_gather | solution.py:73
  7.9 24.7 %copy-start.1 = (f32[2048,128]{1,0:T(8,128)S(1)}, f32[2048,128]{1,0:T(8,128)}, u32[]{:S(2)}) copy-start(f32[2048,128]{1,0:T(8,128)} %param.7) | copy-start | bytes 3145732
  7.9 238.0 %all-reduce.8.cloned.1.call-start = ((), (), s32[]{:S(2)}) async-start(), calls=%async_computation.1 | async-start | bytes 2097152 | tf_op jit(solution)/shard_map/psum | solution.py:35
  8.0 21.9 %collective-permute-start = (f32[2048,128]{1,0:T(8,128)}, f32[2048,128]{1,0:T(8,128)S(1)}, u32[]{:S(2)}, u32[]{:S(2)}) collective-permute-start(f32[2048,128]{1,0:T(8,128)} %param.9), channel_id=1, source_target_pairs={{0,28},{4,0},{8,4},{12,8},{16,12},{20,16},{24,20},{28,24},{1,29},{... | collective-permute-start | bytes 3145736 | tf_op jit(solution)/shard_map/ppermute | solution.py:12
  32.6 1.2 copy-start
  32.6 47.7 %collective-permute-start.1 = (f32[4096,128]{1,0:T(8,128)}, f32[4096,128]{1,0:T(8,128)}, u32[]{:S(2)}, u32[]{:S(2)}) collective-permute-start(f32[4096,128]{1,0:T(8,128)} %pad_maximum_fusion.1), channel_id=1, source_target_pairs={{0,24},{4,28},{8,0},{12,4},{16,8},{20,12},{24,16},{28,20},{1,25},{... | collective-permute-start | bytes 6291464 | tf_op jit(solution)/shard_map/ppermute | solution.py:12
  34.9 12.8 %copy-start.5 = (f32[2048,256]{1,0:T(8,128)}, f32[2048,256]{1,0:T(8,128)S(1)}, u32[]{:S(2)}) copy-start(f32[2048,256]{1,0:T(8,128)S(1)} %get-tuple-element.8) | copy-start | bytes 6291460
  84.1 115.4 %collective-permute-start.2 = (f32[8192,128]{1,0:T(8,128)}, f32[8192,128]{1,0:T(8,128)}, u32[]{:S(2)}, u32[]{:S(2)}) collective-permute-start(f32[8192,128]{1,0:T(8,128)} %pad_maximum_fusion), channel_id=1, source_target_pairs={{0,16},{4,20},{8,24},{12,28},{16,0},{20,4},{24,8},{28,12},{1,17},{... | collective-permute-start | bytes 12582920 | tf_op jit(solution)/shard_map/ppermute | solution.py:12
  191.4 119.4 %all-reduce.14.cloned.1.call-start = ((), (), s32[]{:S(2)}) async-start(), calls=%async_computation.4 | async-start | bytes 4325376 | tf_op jit(solution)/shard_map/psum | solution.py:37
  249.0 190.5 %all-reduce.10.cloned.1.call-start = ((), (), s32[]{:S(2)}) async-start(), calls=%async_computation.2 | async-start | bytes 2097152 | tf_op jit(solution)/shard_map/psum | solution.py:35
  253.5 3.3 copy-start.7
  253.5 3.3 copy-start.9
  310.8 3.6 copy-start.13
  310.8 4.1 copy-start.4
  317.7 33.4 %copy-start.2 = (f32[4096,128]{1,0:T(8,128)S(1)}, f32[4096,128]{1,0:T(8,128)}, u32[]{:S(2)}) copy-start(f32[4096,128]{1,0:T(8,128)} %constant_dynamic-slice_fusion) | copy-start | bytes 6291460
  382.0 131.3 %all-reduce.12.cloned.1.call-start = ((), (), s32[]{:S(2)}) async-start(), calls=%async_computation.3 | async-start | bytes 6553600 | tf_op jit(solution)/shard_map/psum | solution.py:37
  443.1 1.2 copy-start.8
  443.1 1.2 copy-start.10
  513.3 3.6 copy-start.14
  513.3 4.1 copy-start.3
  519.3 1.0 copy-start.12
  519.3 1.6 copy-start.11
  520.3 1.7 copy-start.6
Sparse Core Ops, SparseCore 0:
  9.9 127.2 all-gather.1
  191.5 54.4 all-reduce.7
  249.3 61.4 all-reduce.13
  382.2 51.1 all-reduce.9
  443.3 70.0 all-reduce.11
